TPU v7x, 256 devices: a whole 4x4x8 slice. The times are simulated.
256 devices in a mesh: req: 16 (over y_hi, z), head: 16 (over y_lo, x, core).
Axes of the slice: x: 4, y: 4 (y_hi: 2, y_lo: 2; y = y_hi * 2 + y_lo), z: 8, core: 2. Of those that a mesh axis runs over, the one named last changes fastest.
Arguments:
- queries: bfloat16 [4096, 8192], P('req', 'head'), may hold values from -8 to 8
- new_keys: bfloat16 [4096, 1024], P('req'), may hold values from -5 to 5
- new_values: bfloat16 [4096, 1024], P('req'), may hold values from -24 to 24
- cache_keys: bfloat16 [32, 256, 1024], P('req'), may hold values from -4 to 4
- cache_values: bfloat16 [32, 256, 1024], P('req'), may hold values from -24 to 24
- request_slot: int32 [16], P('req'), may hold values from 0 to 1
- tenant_ids: int32 [4096], P('req'), may hold values from 0 to 255
- out_weight: bfloat16 [8192, 8192], P('req', 'head'), may hold values from -0.0625 to 0.0625
- adapter_down: bfloat16 [8192, 8192], P('head', 'req'), may hold values from -0.0625 to 0.0625
- adapter_up: bfloat16 [8192, 8192], P('req', 'head'), may hold values from -1 to 1
Outputs:
- mixed: bfloat16 [4096, 8192], P('req', 'head')
All inputs are finite; a program needn't handle non-finite values.
Results may differ from a plain program's by a relative error of at most 0.0064.
Values may be sent and summed in bfloat16 or wider, within the bound.
No kernel may reach another device: no remote copies, remote signals or barrier semaphores. Data moves between devices by JAX's collectives and lax.ppermute only.
A program may use at most 128 MiB of HBM per device.

v0:
```python
import jax
import jax.numpy as jnp
from jax import lax
from jax.sharding import PartitionSpec as P

HEADS = 64
HD = 128
KVH = 8
RANK = 32


def pick_heads(block, shared_index):
    spread = block.reshape(block.shape[0], KVH, HD)
    return jnp.take(spread, shared_index, axis=1)


def select(tenants, count):
    return tenants[:, None] == jnp.arange(count, dtype=jnp.int32)[None, :]


def shrink(block, tenants, weights):
    count = weights.shape[1] // RANK
    product = jnp.dot(block, weights, preferred_element_type=jnp.float32)
    product = product.reshape(block.shape[0], count, RANK)
    chosen = select(tenants, count).astype(jnp.float32)
    return jnp.sum(product * chosen[:, :, None], axis=1)


def expand(shrunk, tenants, weights):
    count = weights.shape[0] // RANK
    chosen = select(tenants, count).astype(jnp.bfloat16)
    spread = (chosen[:, :, None] * shrunk[:, None, :]).reshape(shrunk.shape[0], count * RANK)
    return jnp.dot(spread, weights, preferred_element_type=jnp.float32)


def attention(queries, new_keys, new_values, cache_keys, cache_values, request_slot):
    row_count = queries.shape[0]
    local_heads = queries.shape[1] // HD
    group = HEADS // KVH
    shared_index = (
        lax.axis_index("head") * local_heads + jnp.arange(local_heads, dtype=jnp.int32)
    ) // group
    slot_index = request_slot[0]
    keys_old = pick_heads(
        lax.dynamic_index_in_dim(cache_keys, slot_index, 0, keepdims=False), shared_index
    )
    values_old = pick_heads(
        lax.dynamic_index_in_dim(cache_values, slot_index, 0, keepdims=False), shared_index
    )
    keys_new = pick_heads(new_keys, shared_index)
    values_new = pick_heads(new_values, shared_index)
    split_queries = queries.reshape(row_count, local_heads, HD)
    scale = HD ** (-0.5)
    scores_old = (
        jnp.einsum("qhd,khd->hqk", split_queries, keys_old, preferred_element_type=jnp.float32)
        * scale
    )
    scores_new = (
        jnp.einsum("qhd,khd->hqk", split_queries, keys_new, preferred_element_type=jnp.float32)
        * scale
    )
    causal = (
        jnp.arange(row_count, dtype=jnp.int32)[:, None]
        >= jnp.arange(row_count, dtype=jnp.int32)[None, :]
    )
    scores_new = jnp.where(causal[None], scores_new, -1e30)
    highest = jnp.maximum(jnp.max(scores_old, axis=2), jnp.max(scores_new, axis=2))[:, :, None]
    weights_old = jnp.exp(scores_old - highest)
    weights_new = jnp.where(causal[None], jnp.exp(scores_new - highest), 0.0)
    total = jnp.sum(weights_old, axis=2, keepdims=True) + jnp.sum(
        weights_new, axis=2, keepdims=True
    )
    probs_old = (weights_old / total).astype(jnp.bfloat16)
    probs_new = (weights_new / total).astype(jnp.bfloat16)
    output = jnp.einsum("hqk,khd->qhd", probs_old, values_old, preferred_element_type=jnp.float32)
    output = output + jnp.einsum(
        "hqk,khd->qhd", probs_new, values_new, preferred_element_type=jnp.float32
    )
    return output.reshape(row_count, local_heads * HD).astype(jnp.bfloat16)


def local(
    queries,
    new_keys,
    new_values,
    cache_keys,
    cache_values,
    request_slot,
    tenant_ids,
    out_weight,
    adapter_down,
    adapter_up,
):
    attended = attention(queries, new_keys, new_values, cache_keys, cache_values, request_slot)
    partial_value = shrink(
        attended, tenant_ids, lax.all_gather(adapter_down, "req", axis=1, tiled=True)
    )
    shrunk = lax.psum(partial_value, "head").astype(jnp.bfloat16)
    columns = lax.all_gather(out_weight, "req", axis=0, tiled=True)
    rows_block = lax.all_to_all(columns, "head", split_axis=0, concat_axis=1, tiled=True)
    base_term = jnp.dot(attended, rows_block, preferred_element_type=jnp.float32)
    base = lax.psum_scatter(base_term, "head", scatter_dimension=1, tiled=True)
    summed = expand(shrunk, tenant_ids, lax.all_gather(adapter_up, "req", axis=0, tiled=True))
    delta = lax.optimization_barrier(summed.astype(jnp.bfloat16)).astype(jnp.float32)
    return (base + delta).astype(jnp.bfloat16)


def solution(mesh):
    placed = (
        P("req", "head"),
        P("req", None),
        P("req", None),
        P("req", None, None),
        P("req", None, None),
        P("req"),
        P("req"),
        P("req", "head"),
        P("head", "req"),
        P("req", "head"),
    )
    return jax.shard_map(
        local, mesh=mesh, in_specs=placed, out_specs=P("req", "head"), check_vma=False
    )
```

profile of v0, /device:TPU:16, one launch (start us, length us, event | category | flops | bytes accessed | tf_op | source)
XLA Modules:
  0.0 553.8 jit_solution(7732991442768242154)
XLA Ops:
  6.5 0.7 all-gather.4.cloned.1.call-update
  7.3 2.1 copy.41
  9.5 0.7 all-gather.8.cloned.1.call-update
  10.1 135.3 %all-gather.4.cloned.1.call-done = bf16[8192,512]{1,0:T(8,128)(2,1)} async-done(((bf16[512,512]{1,0:T(8,128)(2,1)}), bf16[8192,512]{1,0:T(8,128)(2,1)}) %all-gather.4.cloned.1.call-update) | async-done | bytes 8388624 | tf_op jit(solution)/shard_map/all_gather | solution.py:99
  145.4 6.1 %all-to-all-start = ((bf16[16,512,512]{2,1,0:T(8,128)(2,1)}), bf16[16,512,512]{2,1,0:T(8,128)(2,1)}, u32[]{:S(2)}, u32[]{:S(2)}) async-start(bf16[16,512,512]{2,1,0:T(8,128)(2,1)} %bitcast.65), calls=%async_computation | async-start | bytes 16777216 | tf_op jit(solution)/shard_map/all_to_all | solution.py:100
  152.3 1.1 constant_dynamic-slice_fusion
  154.4 0.6 gather_fusion.1
  155.0 0.6 gather_fusion.2
  156.1 0.6 gather_fusion
  157.2 0.6 gather_fusion.3
  159.0 0.4 fusion.13
  159.4 0.5 fusion.7
  159.9 104.5 %all-to-all-done = bf16[16,512,512]{2,1,0:T(8,128)(2,1)} async-done(((bf16[16,512,512]{2,1,0:T(8,128)(2,1)}), bf16[16,512,512]{2,1,0:T(8,128)(2,1)}, u32[]{:S(2)}, u32[]{:S(2)}) %all-to-all-start) | async-done | bytes 8388640 | tf_op jit(solution)/shard_map/all_to_all | solution.py:100
  264.4 12.3 %copy.40 = bf16[512,16,512]{0,2,1:T(8,128)(2,1)} copy(bf16[512,16,512]{2,0,1:T(8,128)(2,1)} %bitcast.14) | data formatting | bytes 16777216 | tf_op jit(solution)/shard_map/all_to_all | solution.py:100
  276.8 9.0 %fusion.44 = f32[256,8192]{1,0:T(8,128)} fusion(bf16[256,512]{0,1:T(8,128)(2,1)S(1)} %bitcast.70, bf16[512,8192]{0,1:T(8,128)(2,1)} %bitcast.63), kind=kOutput, calls=%fused_computation.68 | convolution fusion | flops 2147483648 | bytes 17039360 | tf_op jit(solution)/shard_map/dot_general | solution.py:101
  285.8 0.7 copy-done.5
  286.5 40.1 %all-gather.6.cloned.1.call-done = bf16[512,8192]{0,1:T(8,128)(2,1)} async-done(((bf16[512,512]{0,1:T(8,128)(2,1)}), bf16[512,8192]{0,1:T(8,128)(2,1)}) %all-gather.6.cloned.1.call-update) | async-done | bytes 8388624 | tf_op jit(solution)/shard_map/all_gather | solution.py:96
  326.6 12.9 %multiply_reduce_fusion = f32[256,32]{0,1:T(8,128)S(1)} fusion(f32[256,256]{0,1:T(8,128)S(1)} %get-tuple-element.9, bf16[256,512,1]{0,1,2:T(8,128)(2,1)S(1)} %bitcast.71, bf16[256,32,512]{2,1,0:T(8,128)(2,1)} %bitcast.72), kind=kOutput, calls=%fused_computation.6 | convolution fusion | flops 2151669760 | bytes 8945664 | tf_op jit(solution)/shard_map/dot_general | solution.py:23
  339.5 58.6 %psum.7 = bf16[256,32]{0,1:T(8,128)(2,1)S(1)} all-reduce(f32[256,32]{0,1:T(8,128)S(1)} %multiply_reduce_fusion), channel_id=1, replica_groups=mesh['req'=16,'head'=16] {'head'}, use_global_device_ids=true, to_apply=%region_6.8 | all-reduce | flops 8192 | bytes 49152 | tf_op jit(solution)/shard_map/psum | solution.py:98
  398.1 2.2 broadcast_multiply_fusion
  400.3 66.4 %all-gather.8.cloned.1.call-done = bf16[8192,512]{1,0:T(8,128)(2,1)} async-done(((bf16[512,512]{1,0:T(8,128)(2,1)}), bf16[8192,512]{1,0:T(8,128)(2,1)}) %all-gather.8.cloned.1.call-update) | async-done | bytes 8388624 | tf_op jit(solution)/shard_map/all_gather | solution.py:103
  466.8 7.0 %convolution_convert_fusion = bf16[256,512]{1,0:T(8,128)(2,1)S(1)} fusion(bf16[256,8192]{0,1:T(8,128)(2,1)} %bitcast.64, bf16[8192,512]{1,0:T(8,128)(2,1)} %all-gather.8.cloned.1.call-done), kind=kOutput, calls=%fused_computation.15 | convolution fusion | flops 2147614720 | bytes 12845056 | tf_op jit(solution)/shard_map/dot_general | solution.py:33
  473.8 71.6 %reduce-scatter.2.cloned.1.call-done = f32[256,512]{1,0:T(8,128)} async-done(((f32[256,8192]{1,0:T(8,128)}), f32[256,512]{1,0:T(8,128)}) %reduce-scatter.2.cloned.1.call-update) | async-done | bytes 524304 | tf_op jit(solution)/shard_map/reduce_scatter | solution.py:102
  545.4 1.8 add_convert_fusion
  (35 shorter events, 3.3 us)
Async XLA Ops:
  6.5 151.3 %copy-start = (bf16[256,512]{1,0:T(8,128)(2,1)S(1)}, bf16[256,512]{1,0:T(8,128)(2,1)}, u32[]{:S(2)}) copy-start(bf16[256,512]{1,0:T(8,128)(2,1)} %param.12) | copy-start | bytes 786436
  6.5 138.9 %all-gather.4.cloned.1.call-start = ((), (), s32[]{:S(2)}) async-start(), calls=%async_computation.2 | async-start | bytes 8912896 | tf_op jit(solution)/shard_map/all_gather | solution.py:99
  7.3 319.3 %all-gather.6.cloned.1.call-start = ((), (), s32[]{:S(2)}) async-start(), calls=%async_computation.4 | async-start | bytes 8912896 | tf_op jit(solution)/shard_map/all_gather | solution.py:96
  9.4 457.3 %all-gather.8.cloned.1.call-start = ((), (), s32[]{:S(2)}) async-start(), calls=%async_computation.5 | async-start | bytes 8912896 | tf_op jit(solution)/shard_map/all_gather | solution.py:103
  145.4 6.8 %copy-start.4 = (bf16[2,256,1024]{2,1,0:T(8,128)(2,1)S(1)}, bf16[2,256,1024]{2,1,0:T(8,128)(2,1)}, u32[]{:S(2)}) copy-start(bf16[2,256,1024]{2,1,0:T(8,128)(2,1)} %param.15) | copy-start | bytes 3145732
  145.4 8.5 %copy-start.2 = (bf16[256,1024]{1,0:T(8,128)(2,1)S(1)}, bf16[256,1024]{1,0:T(8,128)(2,1)}, u32[]{:S(2)}) copy-start(bf16[256,1024]{1,0:T(8,128)(2,1)} %param.13) | copy-start | bytes 1572868
  145.4 119.0 %all-to-all-start = ((bf16[16,512,512]{2,1,0:T(8,128)(2,1)}), bf16[16,512,512]{2,1,0:T(8,128)(2,1)}, u32[]{:S(2)}, u32[]{:S(2)}) async-start(bf16[16,512,512]{2,1,0:T(8,128)(2,1)} %bitcast.65), calls=%async_computation | async-start | bytes 16777216 | tf_op jit(solution)/shard_map/all_to_all | solution.py:100
  151.5 5.2 copy-start.3
  151.5 393.9 %reduce-scatter.2.cloned.1.call-start = ((), (), s32[]{:S(2)}) async-start(), calls=%async_computation.3 | async-start | bytes 8912896 | tf_op jit(solution)/shard_map/reduce_scatter | solution.py:102
  285.8 0.7 copy-start.5
  466.7 80.5 %copy-start.1 = (bf16[256,512]{1,0:T(8,128)(2,1)S(1)}, bf16[256,512]{1,0:T(8,128)(2,1)}, u32[]{:S(2)}) copy-start(bf16[256,512]{1,0:T(8,128)(2,1)} %param.12) | copy-start | bytes 786436
Sparse Core Ops, SparseCore 0:
  9.9 135.4 all-gather.3
  148.0 178.5 all-gather.5
  329.2 137.5 all-gather.7
  469.2 76.2 reduce-scatter.1
where the time goes:
time: 554 us
  waiting for transfers between devices  419 us (76%)
  blocking collectives  58.6 us (11%)
  matrix products  30.6 us (6%)
  local copies, waits for them, and re-layouts  20.5 us (4%)
  between operations  14 us (3%)
  starting transfers between devices  6.19 us (1%)
    all_gather x1, waiting for transfers between devices, local(): columns = lax.all_gather(out_weight, 'req', axis=0, tiled=True)  135 us
    all_to_all x1, waiting for transfers between devices, local(): lax.all_to_all(columns, 'head', split_axis=0, concat_axis=1, tiled=True)  105 us
    reduce_scatter x1, waiting for transfers between devices, local(): base = lax.psum_scatter(base_term, 'head', scatter_dimension=1, tiled=True)  71.6 us
    all_gather x1, waiting for transfers between devices, local(): lax.all_gather(adapter_up, 'req', axis=0, tiled=True)  66.4 us
    psum x1, blocking collectives, local(): shrunk = lax.psum(partial_value, 'head').astype(jnp.bfloat16)  58.6 us
    all_gather x1, waiting for transfers between devices, local(): lax.all_gather(adapter_down, 'req', axis=1, tiled=True)  40.1 us
    dot_general x1, matrix products, shrink(): product = jnp.dot(block, weights, preferred_element_type=jnp.float32)  12.9 us
    all_to_all x1, local copies, waits for them, and re-layouts, local(): lax.all_to_all(columns, 'head', split_axis=0, concat_axis=1, tiled=True)  12.3 us
  transfers between devices with their start and end apart: 5, of which 5 were waited for; matrix products, arithmetic and copies ran while one was open for 10% of the time, Pallas kernels for 0%

commit v1 on v0

--- a/solution.py
+++ b/solution.py
@@ -96,7 +96,10 @@
         attended, tenant_ids, lax.all_gather(adapter_down, "req", axis=1, tiled=True)
     )
     shrunk = lax.psum(partial_value, "head").astype(jnp.bfloat16)
-    columns = lax.all_gather(out_weight, "req", axis=0, tiled=True)
+    size = lax.axis_size("req")
+    blocks = jnp.stack([out_weight for _ in range(size)])
+    blocks = lax.all_to_all(blocks, "req", split_axis=0, concat_axis=0)
+    columns = jnp.concatenate(blocks, axis=0)
     rows_block = lax.all_to_all(columns, "head", split_axis=0, concat_axis=1, tiled=True)
     base_term = jnp.dot(attended, rows_block, preferred_element_type=jnp.float32)
     base = lax.psum_scatter(base_term, "head", scatter_dimension=1, tiled=True)

time: 554 us -> 532 us (0.960)
  waiting for transfers between devices: 419 us -> 391 us
  starting transfers between devices: 6.19 us -> 16.3 us
  local copies, waits for them, and re-layouts: 20.5 us -> 13.5 us
    all_to_all x0 -> x1, waiting for transfers between devices: none -> 218 us  [local(): blocks = lax.all_to_all(blocks, 'req', split_axis=0, concat_axis=0)]
    all_gather x1 -> x0, waiting for transfers between devices: 135 us -> none  [local(): columns = lax.all_gather(out_weight, 'req', axis=0, tiled=True)]
    reduce_scatter x1, waiting for transfers between devices: 71.6 us -> 0.03 us  [local(): base = lax.psum_scatter(base_term, 'head', scatter_dimension=1, tiled=True)]
    all_gather x1, waiting for transfers between devices: 40.1 us -> 0.02 us  [local(): lax.all_gather(adapter_down, 'req', axis=1, tiled=True)]
    all_to_all x1 -> x0, local copies, waits for them, and re-layouts: 12.3 us -> none  [local(): lax.all_to_all(columns, 'head', split_axis=0, concat_axis=1, tiled=True)]
    all_to_all x0 -> x1, starting transfers between devices: none -> 11.4 us  [local(): blocks = lax.all_to_all(blocks, 'req', split_axis=0, concat_axis=0)]
  transfers between devices with their start and end apart: 5 -> 5, of which waited for: 5 -> 3; matrix products, arithmetic and copies ran while one was open for 10% -> 8% of each run, Pallas kernels for 0% -> 0%
where the time goes in v1:
time: 532 us; the launch traced here: 528 us
  waiting for transfers between devices  391 us (73%)
  blocking collectives  56.5 us (11%)
  matrix products  30.6 us (6%)
  starting transfers between devices  16.3 us (3%)
  between operations  15.8 us (3%)
  local copies, waits for them, and re-layouts  13.5 us (3%)
    all_to_all x1, waiting for transfers between devices, local(): blocks = lax.all_to_all(blocks, 'req', split_axis=0, concat_axis=0)  218 us
    all_to_all x1, waiting for transfers between devices, local(): lax.all_to_all(columns, 'head', split_axis=0, concat_axis=1, tiled=True)  104 us
    all_gather x1, waiting for transfers between devices, local(): lax.all_gather(adapter_up, 'req', axis=0, tiled=True)  68.4 us
    psum x1, blocking collectives, local(): shrunk = lax.psum(partial_value, 'head').astype(jnp.bfloat16)  56.5 us
    dot_general x1, matrix products, shrink(): product = jnp.dot(block, weights, preferred_element_type=jnp.float32)  12.9 us
    all_to_all x1, starting transfers between devices, local(): blocks = lax.all_to_all(blocks, 'req', split_axis=0, concat_axis=0)  11.4 us
  transfers between devices with their start and end apart: 5, of which 3 were waited for; matrix products, arithmetic and copies ran while one was open for 8% of the time, Pallas kernels for 0%

profile of v1, /device:TPU:16, one launch (start us, length us, event | category | flops | bytes accessed | tf_op | source)
XLA Modules:
  0.0 528.3 jit_solution(11038765103236102470)
XLA Ops:
  7.4 2.1 copy.42
  9.5 1.3 copy.41
  10.8 4.0 stack.2
  14.8 11.4 %all-to-all-start = ((bf16[16,512,512]{1,2,0:T(8,128)(2,1)}), bf16[16,512,512]{1,2,0:T(8,128)(2,1)}, u32[]{:S(2)}, u32[]{:S(2)}) async-start(bf16[16,512,512]{1,2,0:T(8,128)(2,1)} %stack.2), calls=%async_computation | async-start | bytes 16777216 | tf_op jit(solution)/shard_map/all_to_all | solution.py:101
  26.3 0.7 all-gather.5.cloned.1.call-update
  27.0 217.7 %all-to-all-done = bf16[16,512,512]{1,2,0:T(8,128)(2,1)} async-done(((bf16[16,512,512]{1,2,0:T(8,128)(2,1)}), bf16[16,512,512]{1,2,0:T(8,128)(2,1)}, u32[]{:S(2)}, u32[]{:S(2)}) %all-to-all-start) | async-done | bytes 8388640 | tf_op jit(solution)/shard_map/all_to_all | solution.py:101
  244.7 4.8 all-to-all-start.1
  250.3 1.1 constant_dynamic-slice_fusion
  252.4 0.6 gather_fusion.1
  253.0 0.6 gather_fusion.2
  254.1 0.6 gather_fusion
  255.2 0.6 gather_fusion.3
  256.2 0.4 fusion.43
  257.0 0.4 fusion.13
  257.4 0.5 fusion.7
  257.9 104.3 %all-to-all-done.1 = bf16[16,512,512]{1,2,0:T(8,128)(2,1)} async-done(((bf16[16,512,512]{1,2,0:T(8,128)(2,1)}), bf16[16,512,512]{1,2,0:T(8,128)(2,1)}, u32[]{:S(2)}, u32[]{:S(2)}) %all-to-all-start.1) | async-done | bytes 8388640 | tf_op jit(solution)/shard_map/all_to_all | solution.py:103
  362.2 9.0 %fusion.44 = f32[256,8192]{1,0:T(8,128)} fusion(bf16[256,512]{0,1:T(8,128)(2,1)S(1)} %bitcast.68, bf16[512,8192]{0,1:T(8,128)(2,1)} %bitcast.14), kind=kOutput, calls=%fused_computation.68 | convolution fusion | flops 2147483648 | bytes 17039360 | tf_op jit(solution)/shard_map/dot_general | solution.py:104
  371.2 0.7 copy-done.5
  371.9 12.9 %multiply_reduce_fusion = f32[256,32]{0,1:T(8,128)S(1)} fusion(f32[256,256]{0,1:T(8,128)S(1)} %get-tuple-element.9, bf16[256,512,1]{0,1,2:T(8,128)(2,1)S(1)} %bitcast.69, bf16[256,32,512]{2,1,0:T(8,128)(2,1)} %bitcast.70), kind=kOutput, calls=%fused_computation.6 | convolution fusion | flops 2151669760 | bytes 8945664 | tf_op jit(solution)/shard_map/dot_general | solution.py:23
  384.9 56.5 %psum.7 = bf16[256,32]{0,1:T(8,128)(2,1)S(1)} all-reduce(f32[256,32]{0,1:T(8,128)S(1)} %multiply_reduce_fusion), channel_id=1, replica_groups=mesh['req'=16,'head'=16] {'head'}, use_global_device_ids=true, to_apply=%region_6.8 | all-reduce | flops 8192 | bytes 49152 | tf_op jit(solution)/shard_map/psum | solution.py:98
  441.4 2.2 broadcast_multiply_fusion
  443.6 68.4 %all-gather.5.cloned.1.call-done = bf16[8192,512]{1,0:T(8,128)(2,1)} async-done(((bf16[512,512]{1,0:T(8,128)(2,1)}), bf16[8192,512]{1,0:T(8,128)(2,1)}) %all-gather.5.cloned.1.call-update) | async-done | bytes 8388624 | tf_op jit(solution)/shard_map/all_gather | solution.py:106
  512.0 7.0 %convolution_convert_fusion = bf16[256,512]{1,0:T(8,128)(2,1)S(1)} fusion(bf16[256,8192]{0,1:T(8,128)(2,1)} %bitcast.63, bf16[8192,512]{1,0:T(8,128)(2,1)} %all-gather.5.cloned.1.call-done), kind=kOutput, calls=%fused_computation.15 | convolution fusion | flops 2147614720 | bytes 12845056 | tf_op jit(solution)/shard_map/dot_general | solution.py:33
  519.1 1.8 add_convert_fusion
  (35 shorter events, 2.9 us)
Async XLA Ops:
  7.4 248.5 %copy-start = (bf16[256,512]{1,0:T(8,128)(2,1)S(1)}, bf16[256,512]{1,0:T(8,128)(2,1)}, u32[]{:S(2)}) copy-start(bf16[256,512]{1,0:T(8,128)(2,1)} %param.12) | copy-start | bytes 786436
  7.4 364.6 %all-gather.3.cloned.1.call-start = ((), (), s32[]{:S(2)}) async-start(), calls=%async_computation.4 | async-start | bytes 8912896 | tf_op jit(solution)/shard_map/all_gather | solution.py:96
  14.8 229.9 %all-to-all-start = ((bf16[16,512,512]{1,2,0:T(8,128)(2,1)}), bf16[16,512,512]{1,2,0:T(8,128)(2,1)}, u32[]{:S(2)}, u32[]{:S(2)}) async-start(bf16[16,512,512]{1,2,0:T(8,128)(2,1)} %stack.2), calls=%async_computation | async-start | bytes 16777216 | tf_op jit(solution)/shard_map/all_to_all | solution.py:101
  26.2 485.8 %all-gather.5.cloned.1.call-start = ((), (), s32[]{:S(2)}) async-start(), calls=%async_computation.5 | async-start | bytes 8912896 | tf_op jit(solution)/shard_map/all_gather | solution.py:106
  27.0 223.3 %copy-start.4 = (bf16[2,256,1024]{2,1,0:T(8,128)(2,1)S(1)}, bf16[2,256,1024]{2,1,0:T(8,128)(2,1)}, u32[]{:S(2)}) copy-start(bf16[2,256,1024]{2,1,0:T(8,128)(2,1)} %param.15) | copy-start | bytes 3145732
  27.0 224.9 %copy-start.2 = (bf16[256,1024]{1,0:T(8,128)(2,1)S(1)}, bf16[256,1024]{1,0:T(8,128)(2,1)}, u32[]{:S(2)}) copy-start(bf16[256,1024]{1,0:T(8,128)(2,1)} %param.13) | copy-start | bytes 1572868
  244.7 117.5 %all-to-all-start.1 = ((bf16[16,512,512]{1,2,0:T(8,128)(2,1)}), bf16[16,512,512]{1,2,0:T(8,128)(2,1)}, u32[]{:S(2)}, u32[]{:S(2)}) async-start(bf16[16,512,512]{1,2,0:T(8,128)(2,1)} %all-to-all-done), calls=%async_computation.1 | async-start | bytes 16777216 | tf_op jit(solution)/shard_map/all_to_all | solution.py:103
  249.5 5.2 copy-start.3
  249.5 269.6 %reduce-scatter.2.cloned.1.call-start = ((), (), s32[]{:S(2)}) async-start(), calls=%async_computation.3 | async-start | bytes 8912896 | tf_op jit(solution)/shard_map/reduce_scatter | solution.py:105
  371.2 0.7 copy-start.5
  512.0 8.9 %copy-start.1 = (bf16[256,512]{1,0:T(8,128)(2,1)S(1)}, bf16[256,512]{1,0:T(8,128)(2,1)}, u32[]{:S(2)}) copy-start(bf16[256,512]{1,0:T(8,128)(2,1)} %param.12) | copy-start | bytes 786436
Sparse Core Ops, SparseCore 0:
  10.8 299.6 all-gather.2
  313.0 198.9 all-gather.4
Sparse Core Ops, SparseCore 1:
  371.3 84.1 reduce-scatter.1
